TPU v7x, 32 devices: a whole 2x2x4 slice. The times are simulated.
32 devices in a mesh: dp: 4 (over z), row: 4 (over x, core), col: 2 (over y).
Axes of the slice: x: 2, y: 2, z: 4, core: 2. Of those that a mesh axis runs over, the one named last changes fastest.
Arguments:
- tokens: bfloat16 [11664, 1152], P(('dp', 'col'), 'row'), may hold values from -6 to 6
- ln_gain: bfloat16 [2, 1152], P(None, 'row'), may hold values from 0.5 to 1.5
- ln_bias: bfloat16 [2, 1152], P(None, 'row'), may hold values from -3 to 3
- w_qkv: bfloat16 [1152, 3, 1152], P('row', None, 'col'), may hold values from -0.1875 to 0.1875
- b_qv: bfloat16 [2, 1152], P(None, 'col'), may hold values from -3 to 3
- w_out: bfloat16 [1152, 1152], P('col', 'row'), may hold values from -3 to 3
- b_out: bfloat16 [1152], P('row'), may hold values from -3 to 3
- w_up: bfloat16 [1152, 4304], P('row', 'col'), may hold values from -0.1875 to 0.1875
- b_up: bfloat16 [4304], P('col'), may hold values from -3 to 3
- w_down: bfloat16 [4304, 1152], P('col', 'row'), may hold values from -0.09375 to 0.09375
- b_down: bfloat16 [1152], P('row'), may hold values from -3 to 3
- cotangent: bfloat16 [11664, 1152], P(('dp', 'col'), 'row'), may hold values from -6 to 6
Outputs:
- output: bfloat16 [11664, 1152], P(('dp', 'col'), 'row')
- input_grad: bfloat16 [11664, 1152], P(('dp', 'col'), 'row')
- d_ln_gain: float32 [2, 1152], P(None, 'row')
- d_ln_bias: float32 [2, 1152], P(None, 'row')
- d_w_qkv: float32 [1152, 3, 1152], P(('row', 'dp'), None, 'col')
- d_b_qv: float32 [2, 1152], P(None, 'col')
- d_w_out: float32 [1152, 1152], P(('col', 'dp'), 'row')
- d_b_out: float32 [1152], P('row')
- d_w_up: float32 [1152, 4304], P(('row', 'dp'), 'col')
- d_b_up: float32 [4304], P('col')
- d_w_down: float32 [4304, 1152], P('col', ('row', 'dp'))
- d_b_down: float32 [1152], P('row')
All inputs are finite; a program needn't handle non-finite values.
Results may differ from a plain program's by a relative error of at most 0.018.
Values may be sent and summed in bfloat16 or wider, within the bound.
A program may use at most 192 MiB of HBM per device.

v0:
```python
import jax
import jax.numpy as jnp
from jax import lax
from jax.sharding import PartitionSpec as P

HD = 72
SEQ = 729
epsilon = 1e-06


def gelu_tanh(values):
    return (
        0.5
        * values
        * (1.0 + jnp.tanh(0.7978845608028654 * (values + 0.044715 * values * values * values)))
    )


def row_sums(first_part, second_part):
    return lax.psum((first_part, second_part), "row")


def norm_forward(values, gain, shift):
    full_width = values.shape[1] * lax.axis_size("row")
    row_total, square_total = row_sums(jnp.sum(values, axis=1), jnp.sum(values * values, axis=1))
    row_mean = row_total / full_width
    norm_scale = lax.rsqrt(square_total / full_width - row_mean * row_mean + epsilon)
    normed = (values - row_mean[:, None]) * norm_scale[:, None]
    return (normed, norm_scale, normed * gain + shift)


def norm_backward(incoming, normed, norm_scale, gain):
    full_width = normed.shape[1] * lax.axis_size("row")
    scaled = incoming * gain
    scaled_total, cross_total = row_sums(jnp.sum(scaled, axis=1), jnp.sum(scaled * normed, axis=1))
    back_grad = norm_scale[:, None] * (
        scaled - scaled_total[:, None] / full_width - normed * (cross_total[:, None] / full_width)
    )
    return (back_grad, jnp.sum(incoming * normed, axis=0), jnp.sum(incoming, axis=0))


def gather_tokens(pieces):
    return lax.all_gather(pieces, "col", axis=0, tiled=True)


def sum_over_col(row_term, total_rows):
    return lax.psum_scatter(
        row_term(jnp.int32(0), lax.axis_size("col") * (total_rows // lax.axis_size("col"))),
        "col",
        scatter_dimension=0,
        tiled=True,
    )


def project_in(normed_low, weight):
    rows_all = gather_tokens(normed_low)

    def row_term(first_row, row_count):
        return jnp.dot(rows_all, weight, preferred_element_type=jnp.float32)

    result = lax.psum_scatter(
        row_term(jnp.int32(0), lax.axis_size("row") * (rows_all.shape[0] // lax.axis_size("row"))),
        "row",
        scatter_dimension=0,
        tiled=True,
    )
    return (result, rows_all)


def project_in_back(grad_low, saved_in, weight):
    grads_all = lax.all_gather(grad_low, "row", axis=0, tiled=True)
    weight_grad = lax.dot_general(
        saved_in, grads_all, (((0,), (0,)), ((), ())), preferred_element_type=jnp.float32
    )

    def row_term(first_row, row_count):
        return lax.dot_general(
            grads_all, weight, (((1,), (1,)), ((), ())), preferred_element_type=jnp.float32
        )

    input_grad = sum_over_col(row_term, grads_all.shape[0])
    return (input_grad, weight_grad)


def project_out(inner_low, weight):
    inner_all = lax.all_gather(inner_low, "row", axis=0, tiled=True)

    def row_term(first_row, row_count):
        return jnp.dot(inner_all, weight, preferred_element_type=jnp.float32)

    result = lax.psum_scatter(
        row_term(
            jnp.int32(0), inner_all.shape[0] // lax.axis_size("col") * lax.axis_size("col")
        ).astype(jnp.bfloat16),
        "col",
        scatter_dimension=0,
        tiled=True,
    ).astype(jnp.float32)
    return (result, inner_all)


def project_out_back(grad_low, inner_all, weight):
    grads_all = gather_tokens(grad_low)
    weight_grad = lax.dot_general(
        inner_all, grads_all, (((0,), (0,)), ((), ())), preferred_element_type=jnp.float32
    )
    bias_grad = jnp.sum(grad_low, axis=0, dtype=jnp.float32)

    def row_term(first_row, row_count):
        return lax.dot_general(
            grads_all, weight, (((1,), (1,)), ((), ())), preferred_element_type=jnp.float32
        )

    inner_grad = lax.psum_scatter(
        row_term(jnp.int32(0), lax.axis_size("row") * (grads_all.shape[0] // lax.axis_size("row"))),
        "row",
        scatter_dimension=0,
        tiled=True,
    )
    return (inner_grad, weight_grad, bias_grad)


def attend_forward(image_block):
    queries = image_block[:, 0]
    keys_in = image_block[:, 1]
    values = image_block[:, 2]
    scores = jnp.einsum(
        "qhd,khd->hqk", queries, keys_in, preferred_element_type=jnp.float32
    ) * HD ** (-0.5)
    row_top = jnp.max(scores, axis=-1, keepdims=True)
    exponent = jnp.exp(scores - row_top)
    row_total = jnp.sum(exponent, axis=-1, keepdims=True)
    weights = (exponent / row_total).astype(jnp.bfloat16)
    heads_out = jnp.einsum("hqk,khd->qhd", weights, values, preferred_element_type=jnp.float32)
    return (heads_out.astype(jnp.bfloat16), (row_top + jnp.log(row_total))[..., 0])


def attend_backward(image_block, logsum, grad_heads):
    queries = image_block[:, 0]
    keys_in = image_block[:, 1]
    values = image_block[:, 2]
    scores = jnp.einsum(
        "qhd,khd->hqk", queries, keys_in, preferred_element_type=jnp.float32
    ) * HD ** (-0.5)
    soft_probs = jnp.exp(scores - logsum[..., None])
    weights = soft_probs.astype(jnp.bfloat16)
    value_grad = jnp.einsum("hqk,qhd->khd", weights, grad_heads, preferred_element_type=jnp.float32)
    prob_grad = jnp.einsum("qhd,khd->hqk", grad_heads, values, preferred_element_type=jnp.float32)
    row_delta = jnp.sum(soft_probs * prob_grad, axis=-1, keepdims=True)
    score_grad = (soft_probs * (prob_grad - row_delta)).astype(jnp.bfloat16)
    query_grad = jnp.einsum(
        "hqk,khd->qhd", score_grad, keys_in, preferred_element_type=jnp.float32
    ) * HD ** (-0.5)
    key_grad = jnp.einsum(
        "hqk,qhd->khd", score_grad, queries, preferred_element_type=jnp.float32
    ) * HD ** (-0.5)
    return jnp.stack([query_grad, key_grad, value_grad], axis=1).astype(jnp.bfloat16)


def place_block(block, position, part_count):
    block_size = block.shape[-1]
    zero_vector = jnp.zeros(block.shape[:-1] + (block_size * part_count,), jnp.float32)
    return lax.dynamic_update_slice_in_dim(
        zero_vector, block, position * block_size, block.ndim - 1
    )


def take_block(whole_vector, position, block_size):
    return lax.dynamic_slice_in_dim(
        whole_vector, position * block_size, block_size, whole_vector.ndim - 1
    )


def shards(
    tokens, ln_gain, ln_bias, w_qkv, b_qv, w_out, b_out, w_up, b_up, w_down, b_down, cotangent
):
    inputs = tokens.astype(jnp.float32)
    gain_rows = ln_gain.astype(jnp.float32)
    shift_rows = ln_bias.astype(jnp.float32)
    row_width = tokens.shape[1]
    head_width = b_qv.shape[1]
    heads_here = head_width // HD
    qkv_weight = w_qkv.reshape(row_width, 3 * head_width)
    normed_one, scale_one, first_out = norm_forward(inputs, gain_rows[0], shift_rows[0])
    projected, saved_one = project_in(first_out.astype(jnp.bfloat16), qkv_weight)
    qv_bias = b_qv.astype(jnp.float32)
    bias_rows = jnp.stack([qv_bias[0], jnp.zeros_like(qv_bias[0]), qv_bias[1]])
    images = projected.shape[0] // SEQ
    triple = (projected.reshape(-1, 3, head_width) + bias_rows).astype(jnp.bfloat16)
    triple = triple.reshape(images, SEQ, 3, heads_here, HD)
    heads_low, logsum = lax.map(attend_forward, triple)
    heads_low = heads_low.reshape(-1, head_width)
    attn_part, heads_all = project_out(heads_low, w_out)
    residual = inputs + attn_part + b_out.astype(jnp.float32)
    normed_two, scale_two, second_out = norm_forward(residual, gain_rows[1], shift_rows[1])
    up_total, saved_two = project_in(second_out.astype(jnp.bfloat16), w_up)
    up_value = up_total + b_up.astype(jnp.float32)
    hidden_act, gelu_pull = jax.vjp(gelu_tanh, up_value)
    down_part, hidden_all = project_out(hidden_act.astype(jnp.bfloat16), w_down)
    output = (residual + down_part + b_down.astype(jnp.float32)).astype(jnp.bfloat16)
    act_grad, down_grad, down_bias_grad = project_out_back(cotangent, hidden_all, w_down)
    up_grad = gelu_pull(act_grad)[0].astype(jnp.bfloat16)
    up_bias_grad = jnp.sum(up_grad, axis=0, dtype=jnp.float32)
    second_grad, up_weight_grad = project_in_back(up_grad, saved_two, w_up)
    back_two, gain_two, shift_two = norm_backward(second_grad, normed_two, scale_two, gain_rows[1])
    residual_grad = cotangent.astype(jnp.float32) + back_two
    heads_grad, out_grad, out_bias_grad = project_out_back(
        residual_grad.astype(jnp.bfloat16), heads_all, w_out
    )
    heads_grad = heads_grad.astype(jnp.bfloat16).reshape(images, SEQ, heads_here, HD)
    triple_grad = lax.map(
        lambda image_set: attend_backward(image_set[0], image_set[1], image_set[2]),
        (triple, logsum, heads_grad),
    )
    triple_grad = triple_grad.reshape(-1, 3 * head_width)
    triple_bias_grad = jnp.sum(triple_grad.reshape(-1, 3, head_width), axis=0, dtype=jnp.float32)
    first_grad, triple_weight_grad = project_in_back(triple_grad, saved_one, qkv_weight)
    back_one, gain_one, shift_one = norm_backward(first_grad, normed_one, scale_one, gain_rows[0])
    input_grad = (residual_grad + back_one).astype(jnp.bfloat16)
    row_here = lax.axis_index("row")
    col_here = lax.axis_index("col")
    row_block = jnp.stack([gain_one, gain_two, shift_one, shift_two, out_bias_grad, down_bias_grad])
    row_full = place_block(row_block, row_here, lax.axis_size("row"))
    qv_full = place_block(triple_bias_grad[::2], col_here, lax.axis_size("col"))
    up_full = place_block(up_bias_grad, col_here, lax.axis_size("col"))
    row_summed, qv_summed, up_summed = lax.psum((row_full, qv_full, up_full), ("dp", "row", "col"))
    row_vectors = take_block(row_summed, row_here, row_width)
    qv_vectors = take_block(qv_summed, col_here, head_width)
    up_vector = take_block(up_summed, col_here, up_bias_grad.shape[0])
    triple_shaped = triple_weight_grad.reshape(row_width, 3, head_width)
    triple_total, out_total, up_weight_total, down_total = (
        lax.psum_scatter(
            triple_shaped.astype(jnp.bfloat16), "dp", scatter_dimension=0, tiled=True
        ).astype(jnp.float32),
        lax.psum_scatter(
            out_grad.astype(jnp.bfloat16), "dp", scatter_dimension=0, tiled=True
        ).astype(jnp.float32),
        lax.psum_scatter(
            up_weight_grad.astype(jnp.bfloat16), "dp", scatter_dimension=0, tiled=True
        ).astype(jnp.float32),
        lax.psum_scatter(
            down_grad.astype(jnp.bfloat16), "dp", scatter_dimension=1, tiled=True
        ).astype(jnp.float32),
    )
    return (
        output,
        input_grad,
        row_vectors[0:2],
        row_vectors[2:4],
        triple_total,
        qv_vectors,
        out_total,
        row_vectors[4],
        up_weight_total,
        up_vector,
        down_total,
        row_vectors[5],
    )


def solution(mesh):
    placed = (
        P(("dp", "col"), "row"),
        P(None, "row"),
        P(None, "row"),
        P("row", None, "col"),
        P(None, "col"),
        P("col", "row"),
        P("row"),
        P("row", "col"),
        P("col"),
        P("col", "row"),
        P("row"),
        P(("dp", "col"), "row"),
    )
    return jax.shard_map(
        shards,
        mesh=mesh,
        in_specs=placed,
        out_specs=(
            P(("dp", "col"), "row"),
            P(("dp", "col"), "row"),
            P(None, "row"),
            P(None, "row"),
            P(("row", "dp"), None, "col"),
            P(None, "col"),
            P(("col", "dp"), "row"),
            P("row"),
            P(("row", "dp"), "col"),
            P("col"),
            P("col", ("row", "dp")),
            P("row"),
        ),
        check_vma=False,
    )
```

profile of v0, /device:TPU:0, one launch (start us, length us, event | category | flops | bytes accessed | tf_op | source)
XLA Modules:
  0.0 1888.4 jit_solution(2578188602203052811)
XLA Ops:
  10.2 12.7 all-reduce.18
  27.7 28.1 %all-gather.17.cloned.1.call-done = bf16[2,1458,288]{1,2,0:T(8,128)(2,1)} async-done(((bf16[1,1458,288]{1,2,0:T(8,128)(2,1)}), bf16[2,1458,288]{1,2,0:T(8,128)(2,1)}) %all-gather.17.cloned.1.call-update) | async-done | bytes 1679632 | tf_op jit(solution)/shard_map/all_gather | solution.py:43
  64.9 12.0 fusion.47
  76.9 181.4 %fusion = f32[736,1728]{1,0:T(8,128)} fusion(f32[2916,1728]{1,0:T(8,128)} %fusion.47), kind=kCustom, calls=%all-reduce-scatter | all-reduce-scatter fusion | flops 5087233 | bytes 25243136
  262.4 14.1 concatenate.2
  317.7 32.9 %all-gather.19.cloned.1.call-done = bf16[4,729,576]{1,2,0:T(8,128)(2,1)} async-done(((bf16[1,729,576]{1,2,0:T(8,128)(2,1)}), bf16[4,729,576]{1,2,0:T(8,128)(2,1)}) %all-gather.19.cloned.1.call-update) | async-done | bytes 3359248 | tf_op jit(solution)/shard_map/all_gather | solution.py:86
  387.4 13.8 fusion.49
  401.2 36.7 %all-reduce.26.cloned.1.call-done = bf16[2916,288]{0,1:T(8,128)(2,1)} async-done(((bf16[2916,288]{0,1:T(8,128)(2,1)}), bf16[2916,288]{0,1:T(8,128)(2,1)}) %all-reduce.26.cloned.1.call-update) | async-done | bytes 1679632
  454.0 218.1 %fusion.2 = f32[736,2152]{1,0:T(8,128)} fusion(f32[2916,2152]{1,0:T(8,128)} %fusion.49), kind=kCustom, calls=%all-reduce-scatter.2 | all-reduce-scatter fusion | flops 6335489 | bytes 31436928
  684.4 13.3 fusion.48
  697.7 219.8 %fusion.1 = f32[736,2152]{1,0:T(8,128)} fusion(f32[2916,2152]{1,0:T(8,128)} %fusion.48), kind=kCustom, calls=%all-reduce-scatter.1 | all-reduce-scatter fusion | flops 6335489 | bytes 31436928
  919.8 17.6 concatenate.4
  937.4 17.6 concatenate.3
  968.0 82.1 %all-gather.27.cloned.1.call-done = bf16[4,729,2152]{2,1,0:T(8,128)(2,1)} async-done(((bf16[1,729,2152]{2,1,0:T(8,128)(2,1)}), bf16[4,729,2152]{2,1,0:T(8,128)(2,1)}) %all-gather.27.cloned.1.call-update) | async-done | bytes 12550480 | tf_op jit(solution)/shard_map/all_gather | solution.py:71
  1050.1 18.0 reshape.103
  1079.0 56.0 %all-gather.23.cloned.1.call-done = bf16[4,729,2152]{2,1,0:T(8,128)(2,1)} async-done(((bf16[1,729,2152]{2,1,0:T(8,128)(2,1)}), bf16[4,729,2152]{2,1,0:T(8,128)(2,1)}) %all-gather.23.cloned.1.call-update) | async-done | bytes 12550480 | tf_op jit(solution)/shard_map/all_gather | solution.py:86
  1135.0 17.4 reshape.99
  1152.5 13.6 convolution_convert_fusion.2
  1166.2 62.4 %all-reduce.30.cloned.1.call-done = f32[2916,288]{0,1:T(8,128)} async-done(((f32[2916,288]{0,1:T(8,128)}), f32[2916,288]{0,1:T(8,128)}) %all-reduce.30.cloned.1.call-update) | async-done | bytes 3359248
  1243.3 41.8 %all-reduce.28.cloned.1.call-done = bf16[2916,288]{0,1:T(8,128)(2,1)} async-done(((bf16[2916,288]{0,1:T(8,128)(2,1)}), bf16[2916,288]{0,1:T(8,128)(2,1)}) %all-reduce.28.cloned.1.call-update) | async-done | bytes 1679632
  1293.5 28.9 %all-gather.29.cloned.1.call-done = bf16[2,1458,288]{1,2,0:T(8,128)(2,1)} async-done(((bf16[1,1458,288]{1,2,0:T(8,128)(2,1)}), bf16[2,1458,288]{1,2,0:T(8,128)(2,1)}) %all-gather.29.cloned.1.call-update) | async-done | bytes 1679632 | tf_op jit(solution)/shard_map/all_gather | solution.py:43
  1338.5 120.7 %all-reduce.35 = bf16[2916,576]{0,1:T(8,128)(2,1)} all-reduce(f32[2916,576]{0,1:T(8,128)} %fusion.51), channel_id=8, replica_groups=mesh['dp'=4,'row'=4,'col'=2] {'row'}, use_global_device_ids=true, to_apply=%region_20.21.clone | all-reduce | flops 1679616 | bytes 10077696
  1460.8 12.3 multiply_reduce_fusion
  1473.1 12.8 multiply_convert_fusion
  1515.5 11.8 convolution_convert_fusion
  1532.8 42.1 %all-gather.31.cloned.1.call-done = bf16[4,729,1728]{2,1,0:T(8,128)(2,1)} async-done(((bf16[1,729,1728]{2,1,0:T(8,128)(2,1)}), bf16[4,729,1728]{2,1,0:T(8,128)(2,1)}) %all-gather.31.cloned.1.call-update) | async-done | bytes 10077712 | tf_op jit(solution)/shard_map/all_gather | solution.py:71
  1574.9 14.8 reshape.107
  1619.4 19.5 %reduce-scatter.23.cloned.1.call-done = bf16[2152,72]{0,1:T(8,128)(2,1)} async-done(((bf16[2152,288]{0,1:T(8,128)(2,1)}), bf16[2152,72]{0,1:T(8,128)(2,1)}) %reduce-scatter.23.cloned.1.call-update) | async-done | bytes 309904
  1642.8 19.0 %reduce-scatter.19.cloned.1.call-done = bf16[144,288]{1,0:T(8,128)(2,1)} async-done(((bf16[576,288]{1,0:T(8,128)(2,1)}), bf16[144,288]{1,0:T(8,128)(2,1)}) %reduce-scatter.19.cloned.1.call-update) | async-done | bytes 82960 | tf_op jit(solution)/shard_map/reduce_scatter | solution.py:235
  1663.4 64.7 %all-reduce.34.cloned.1.call-done = bf16[288,3,576]{2,1,0:T(4,128)(2,1)} async-done(((bf16[288,3,576]{2,1,0:T(4,128)(2,1)}), bf16[288,3,576]{2,1,0:T(4,128)(2,1)}) %all-reduce.34.cloned.1.call-update) | async-done | bytes 995344
  1730.0 90.7 %all-reduce.32.cloned.1.call-done = f32[2916,288]{0,1:T(8,128)} async-done(((f32[2916,288]{0,1:T(8,128)}), f32[2916,288]{0,1:T(8,128)}) %all-reduce.32.cloned.1.call-update) | async-done | bytes 3359248
  1823.7 40.5 %all-reduce.14 = (f32[6,1152]{1,0:T(8,128)S(1)}, f32[2,1152]{1,0:T(2,128)S(1)}, f32[4304]{0:T(1024)S(1)}) all-reduce(f32[6,1152]{1,0:T(8,128)S(1)} %dynamic_update_slice.18, f32[2,1152]{1,0:T(2,128)S(1)} %dynamic_update_slice.19, f32[4304]{0:T(1024)S(1)} %dynamic_update_slice.20), channel_id=1, replica_groups=mesh['dp'=4,'row'=4,'col'=2] {'dp','row','col'}, use_global_device_ids=true, to_apply=%region_33.34 | all-reduce | flops 13520 | bytes 108160 | tf_op jit(solution)/shard_map/psum | solution.py:226
  (183 shorter events, 283.8 us)
Async XLA Ops:
  7.2 677.2 %copy-start = (bf16[288,2152]{1,0:T(8,128)(2,1)S(1)}, bf16[288,2152]{1,0:T(8,128)(2,1)}, u32[]{:S(2)}) copy-start(bf16[288,2152]{1,0:T(8,128)(2,1)} %param.19) | copy-start | bytes 3718660
  7.2 18.9 copy-start.10
  7.2 48.7 %all-gather.17.cloned.1.call-start = ((), (), s32[]{:S(2)}) async-start(), calls=%async_computation.4 | async-start | bytes 2654208 | tf_op jit(solution)/shard_map/all_gather | solution.py:43
  8.8 18.9 %copy-start.18 = (bf16[2,576]{1,0:T(2,128)(2,1)S(1)}, bf16[2,576]{1,0:T(2,128)(2,1)}, u32[]{:S(2)}) copy-start(bf16[2,576]{1,0:T(2,128)(2,1)} %param.16) | copy-start | bytes 6916
  26.0 324.6 %all-gather.19.cloned.1.call-start = ((), (), s32[]{:S(2)}) async-start(), calls=%async_computation.5 | async-start | bytes 4423680 | tf_op jit(solution)/shard_map/all_gather | solution.py:86
  76.9 184.3 %copy-start.20 = (u32[32]{0:T(128)S(1)}, u32[32]{0:T(128)}, u32[]{:S(2)}) copy-start(u32[32]{0:T(128)} %constant.88) | copy-start | bytes 388
  259.2 3.2 collective-permute-start
  316.9 64.7 %all-gather.25.cloned.1.call-start = ((), (), s32[]{:S(2)}) async-start(), calls=%async_computation.8 | async-start | bytes 2654208 | tf_op jit(solution)/shard_map/all_gather | solution.py:43
  317.6 120.3 %all-reduce.26.cloned.1.call-start = ((), (), s32[]{:S(2)}) async-start(), calls=%async_computation.12 | async-start | bytes 3391488
  369.7 304.9 %all-gather.21.cloned.1.call-start = ((), (), s32[]{:S(2)}) async-start(), calls=%async_computation.6 | async-start | bytes 2654208 | tf_op jit(solution)/shard_map/all_gather | solution.py:43
  387.4 50.6 %copy-start.2 = (bf16[1458,288]{0,1:T(8,128)(2,1)S(1)}, bf16[1458,288]{0,1:T(8,128)(2,1)}, u32[]{:S(2)}) copy-start(bf16[1458,288]{0,1:T(8,128)(2,1)} %param.12) | copy-start | bytes 2519428
  453.9 596.1 %all-gather.27.cloned.1.call-start = ((), (), s32[]{:S(2)}) async-start(), calls=%async_computation.9 | async-start | bytes 16015360 | tf_op jit(solution)/shard_map/all_gather | solution.py:71
  673.0 246.8 %collective-permute-start.2 = (f32[21,2152]{1,0:T(8,128)S(1)}, f32[21,2152]{1,0:T(8,128)S(1)}, u32[]{:S(2)}, u32[]{:S(2)}) collective-permute-start(f32[21,2152]{1,0:T(8,128)S(1)} %slice.78), channel_id=1, source_target_pairs={{0,2},{2,4},{4,6},{1,3},{3,5},{5,7},{8,10},{10,12},{12,14},{9,11},... | collective-permute-start | bytes 542312
  697.7 222.1 %copy-start.19 = (bf16[2152]{0:T(1024)(128)(2,1)S(1)}, bf16[2152]{0:T(1024)(128)(2,1)}, u32[]{:S(2)}) copy-start(bf16[2152]{0:T(1024)(128)(2,1)} %param.20) | copy-start | bytes 12916
  918.5 19.0 %collective-permute-start.1 = (f32[21,2152]{1,0:T(8,128)S(1)}, f32[21,2152]{1,0:T(8,128)S(1)}, u32[]{:S(2)}, u32[]{:S(2)}) collective-permute-start(f32[21,2152]{1,0:T(8,128)S(1)} %slice.77), channel_id=1, source_target_pairs={{0,2},{2,4},{4,6},{1,3},{3,5},{5,7},{8,10},{10,12},{12,14},{9,11},... | collective-permute-start | bytes 542312
  966.8 168.3 %all-gather.23.cloned.1.call-start = ((), (), s32[]{:S(2)}) async-start(), calls=%async_computation.7 | async-start | bytes 16015360 | tf_op jit(solution)/shard_map/all_gather | solution.py:86
  967.5 261.1 %all-reduce.30.cloned.1.call-start = ((), (), s32[]{:S(2)}) async-start(), calls=%async_computation.14 | async-start | bytes 6782976
  1078.8 73.7 %copy-start.9 = (bf16[2152,288]{0,1:T(8,128)(2,1)S(1)}, bf16[2152,288]{0,1:T(8,128)(2,1)}, u32[]{:S(2)}) copy-start(bf16[2152,288]{0,1:T(8,128)(2,1)} %param.21) | copy-start | bytes 3718660
  1078.8 206.3 %all-reduce.28.cloned.1.call-start = ((), (), s32[]{:S(2)}) async-start(), calls=%async_computation.13 | async-start | bytes 3391488
  1152.5 13.7 copy-start.22
  1166.1 119.0 %copy-start.8 = (bf16[1458,288]{0,1:T(8,128)(2,1)S(1)}, bf16[1458,288]{0,1:T(8,128)(2,1)}, u32[]{:S(2)}) copy-start(bf16[1458,288]{0,1:T(8,128)(2,1)} %param.23) | copy-start | bytes 2519428
  1166.1 156.3 %all-gather.29.cloned.1.call-start = ((), (), s32[]{:S(2)}) async-start(), calls=%async_computation.10 | async-start | bytes 2654208 | tf_op jit(solution)/shard_map/all_gather | solution.py:43
  1292.8 282.1 %all-gather.31.cloned.1.call-start = ((), (), s32[]{:S(2)}) async-start(), calls=%async_computation.11 | async-start | bytes 13189120 | tf_op jit(solution)/shard_map/all_gather | solution.py:71
  1473.1 12.8 copy-start.4
  1504.7 112.9 %reduce-scatter.21.cloned.1.call-start = ((), (), s32[]{:S(2)}) async-start(), calls=%async_computation.17 | async-start | bytes 1566720
  1515.4 123.5 %reduce-scatter.23.cloned.1.call-start = ((), (), s32[]{:S(2)}) async-start(), calls=%async_computation.18 | async-start | bytes 1566720
  1527.3 134.5 %reduce-scatter.19.cloned.1.call-start = ((), (), s32[]{:S(2)}) async-start(), calls=%async_computation.3 | async-start | bytes 552960 | tf_op jit(solution)/shard_map/reduce_scatter | solution.py:235
  1532.6 195.5 %all-reduce.34.cloned.1.call-start = ((), (), s32[]{:S(2)}) async-start(), calls=%async_computation.16 | async-start | bytes 2949120
  1605.5 215.2 %all-reduce.32.cloned.1.call-start = ((), (), s32[]{:S(2)}) async-start(), calls=%async_computation.15 | async-start | bytes 6782976
  1640.8 180.0 %copy-start.13 = (f32[1458]{0:T(1024)S(1)}, f32[1458]{0:T(1024)}, u32[]{:S(2)}) copy-start(f32[1458]{0:T(1024)} %copy-done.12) | copy-start | bytes 17500
  1640.8 180.0 %copy-start.15 = (f32[1458]{0:T(1024)S(1)}, f32[1458]{0:T(1024)}, u32[]{:S(2)}) copy-start(f32[1458]{0:T(1024)} %copy-done.14) | copy-start | bytes 17500
  1640.8 179.9 %copy-start.17 = (f32[288]{0:T(512)S(1)}, f32[288]{0:T(512)}, u32[]{:S(2)}) copy-start(f32[288]{0:T(512)} %copy-done.16) | copy-start | bytes 3460
  (12 other events, 48.0 us)
Sparse Core Ops, SparseCore 0:
  26.1 29.7 all-gather.16
  317.0 33.4 all-gather.18
  352.1 29.3 all-gather.24
  383.7 54.1 all-reduce.25
  454.1 29.0 all-gather.20
  966.9 83.1 all-gather.26
  1051.6 83.3 all-gather.22
  1137.4 91.1 all-reduce.29
  1230.9 54.1 all-reduce.27
  1292.9 29.4 all-gather.28
  1504.8 70.0 all-gather.30
  1577.1 30.2 reduce-scatter.20
  1609.7 29.1 reduce-scatter.22
  1641.6 20.1 reduce-scatter.18
  1664.0 64.0 all-reduce.33
  1730.3 90.4 all-reduce.31
where the time goes:
time: 1900 us; the launch traced here: 1890 us
  blocking collectives  826 us (43%)
  waiting for transfers between devices  617 us (32%)
  local copies, waits for them, and re-layouts  186 us (10%)
  matrix products  162 us (9%)
  other arithmetic  73.3 us (4%)
    unnamed x4, blocking collectives  740 us
    unnamed x26, waiting for transfers between devices  317 us
    unnamed x71, local copies, waits for them, and re-layouts  144 us
    all_gather x2, waiting for transfers between devices, project_in_back(): grads_all = lax.all_gather(grad_low, 'row', axis=0, tiled=True)  124 us
    all_gather x2, waiting for transfers between devices, project_out(): inner_all = lax.all_gather(inner_low, 'row', axis=0, tiled=True)  88.9 us
    all_gather x4, waiting for transfers between devices, gather_tokens(): return lax.all_gather(pieces, 'col', axis=0, tiled=True)  67.5 us
    psum x4, blocking collectives, row_sums(): return lax.psum((first_part, second_part), 'row')  45.8 us
    psum x1, blocking collectives, shards(): lax.psum((row_full, qv_full, up_full), ('dp', 'row', 'col'))  40.5 us
  transfers between devices with their start and end apart: 19, of which 14 were waited for; matrix products, arithmetic and copies ran while one was open for 35% of the time, Pallas kernels for 0%

commit v1 on v0

--- a/solution.py
+++ b/solution.py
@@ -83,7 +83,14 @@
 
 
 def project_out(inner_low, weight):
-    inner_all = lax.all_gather(inner_low, "row", axis=0, tiled=True)
+    ways, here = (lax.axis_size("row"), lax.axis_index("row"))
+    inner_all, reach = (inner_low, 1)
+    while reach < ways:
+        theirs = lax.ppermute(inner_all, "row", [(d, d ^ reach) for d in range(ways)])
+        mine_first = jnp.concatenate([inner_all, theirs], axis=0)
+        theirs_first = jnp.concatenate([theirs, inner_all], axis=0)
+        inner_all = jnp.where(here & reach == 0, mine_first, theirs_first)
+        reach = 2 * reach
 
     def row_term(first_row, row_count):
         return jnp.dot(inner_all, weight, preferred_element_type=jnp.float32)

time: 1900 us -> 1890 us (level)
  local copies, waits for them, and re-layouts: 186 us -> 154 us
    ppermute x0 -> x4, waiting for transfers between devices: none -> 91.6 us  [project_out(): lax.ppermute(inner_all, 'row', [(d, d ^ reach) for d in range(ways)])]
    all_gather x2 -> x0, waiting for transfers between devices: 88.9 us -> none  [project_out(): inner_all = lax.all_gather(inner_low, 'row', axis=0, tiled=True)]
    all_gather x2, waiting for transfers between devices: 124 us -> 164 us  [project_in_back(): grads_all = lax.all_gather(grad_low, 'row', axis=0, tiled=True)]
    unnamed x26 -> x24, waiting for transfers between devices: 317 us -> 281 us
    unnamed x71 -> x75, local copies, waits for them, and re-layouts: 144 us -> 119 us
  transfers between devices with their start and end apart: 19 -> 21, of which waited for: 14 -> 15; matrix products, arithmetic and copies ran while one was open for 35% -> 35% of each run, Pallas kernels for 0% -> 0%
where the time goes in v1:
time: 1890 us; the launch traced here: 1880 us
  blocking collectives  826 us (44%)
  waiting for transfers between devices  613 us (32%)
  matrix products  171 us (9%)
  local copies, waits for them, and re-layouts  154 us (8%)
  other arithmetic  86.1 us (5%)
    unnamed x4, blocking collectives  740 us
    unnamed x24, waiting for transfers between devices  281 us
    all_gather x2, waiting for transfers between devices, project_in_back(): grads_all = lax.all_gather(grad_low, 'row', axis=0, tiled=True)  164 us
    unnamed x75, local copies, waits for them, and re-layouts  119 us
    ppermute x4, waiting for transfers between devices, project_out(): lax.ppermute(inner_all, 'row', [(d, d ^ reach) for d in range(ways)])  91.6 us
    all_gather x4, waiting for transfers between devices, gather_tokens(): return lax.all_gather(pieces, 'col', axis=0, tiled=True)  57.1 us
    psum x4, blocking collectives, row_sums(): return lax.psum((first_part, second_part), 'row')  45.5 us
    psum x1, blocking collectives, shards(): lax.psum((row_full, qv_full, up_full), ('dp', 'row', 'col'))  40.5 us
  transfers between devices with their start and end apart: 21, of which 15 were waited for; matrix products, arithmetic and copies ran while one was open for 35% of the time, Pallas kernels for 0%

profile of v1, /device:TPU:0, one launch (start us, length us, event | category | flops | bytes accessed | tf_op | source)
XLA Modules:
  0.0 1881.0 jit_solution(10700760694007215343)
XLA Ops:
  10.2 12.7 all-reduce.18
  27.7 28.1 %all-gather.13.cloned.1.call-done = bf16[2,1458,288]{1,2,0:T(8,128)(2,1)} async-done(((bf16[1,1458,288]{1,2,0:T(8,128)(2,1)}), bf16[2,1458,288]{1,2,0:T(8,128)(2,1)}) %all-gather.13.cloned.1.call-update) | async-done | bytes 1679632 | tf_op jit(solution)/shard_map/all_gather | solution.py:43
  64.9 12.0 fusion.50
  76.9 181.5 %fusion = f32[736,1728]{1,0:T(8,128)} fusion(f32[2916,1728]{1,0:T(8,128)} %fusion.50), kind=kCustom, calls=%all-reduce-scatter | all-reduce-scatter fusion | flops 5087233 | bytes 25243136
  262.5 14.1 concatenate.34
  326.4 38.9 %collective-permute-done.1 = bf16[1458,576]{0,1:T(8,128)(2,1)} collective-permute-done((bf16[1458,576]{0,1:T(8,128)(2,1)S(1)}, bf16[1458,576]{0,1:T(8,128)(2,1)}, u32[]{:S(2)}, u32[]{:S(2)}) %collective-permute-start.1) | collective-permute-done | bytes 1679648 | tf_op jit(solution)/shard_map/ppermute | solution.py:89
  378.2 13.9 fusion.52
  392.1 33.4 %all-reduce.26.cloned.1.call-done = bf16[2916,288]{0,1:T(8,128)(2,1)} async-done(((bf16[2916,288]{0,1:T(8,128)(2,1)}), bf16[2916,288]{0,1:T(8,128)(2,1)}) %all-reduce.26.cloned.1.call-update) | async-done | bytes 1679632
  441.6 218.2 %fusion.2 = f32[736,2152]{1,0:T(8,128)} fusion(f32[2916,2152]{1,0:T(8,128)} %fusion.52), kind=kCustom, calls=%all-reduce-scatter.2 | all-reduce-scatter fusion | flops 6335489 | bytes 31436928
  672.1 13.1 fusion.51
  685.3 219.9 %fusion.1 = f32[736,2152]{1,0:T(8,128)} fusion(f32[2916,2152]{1,0:T(8,128)} %fusion.51), kind=kCustom, calls=%all-reduce-scatter.1 | all-reduce-scatter fusion | flops 6335489 | bytes 31436928
  907.5 17.6 concatenate.36
  925.1 17.5 concatenate.35
  942.6 12.3 convert_reduce_fusion
  971.4 128.7 %all-gather.19.cloned.1.call-done = bf16[4,729,2152]{2,1,0:T(8,128)(2,1)} async-done(((bf16[1,729,2152]{2,1,0:T(8,128)(2,1)}), bf16[4,729,2152]{2,1,0:T(8,128)(2,1)}) %all-gather.19.cloned.1.call-update) | async-done | bytes 12550480 | tf_op jit(solution)/shard_map/all_gather | solution.py:71
  1100.1 16.9 reshape.99
  1127.9 44.9 %collective-permute-done.3 = bf16[1458,2152]{1,0:T(8,128)(2,1)} collective-permute-done((bf16[1458,2152]{1,0:T(8,128)(2,1)}, bf16[1458,2152]{1,0:T(8,128)(2,1)}, u32[]{:S(2)}, u32[]{:S(2)}) %collective-permute-start.3) | collective-permute-done | bytes 6275264 | tf_op jit(solution)/shard_map/ppermute | solution.py:89
  1172.9 17.1 convolution_convert_fusion.2
  1190.0 30.3 %all-reduce.30.cloned.1.call-done = f32[2916,288]{0,1:T(8,128)} async-done(((f32[2916,288]{0,1:T(8,128)}), f32[2916,288]{0,1:T(8,128)}) %all-reduce.30.cloned.1.call-update) | async-done | bytes 3359248
  1234.8 42.1 %all-reduce.28.cloned.1.call-done = bf16[2916,288]{0,1:T(8,128)(2,1)} async-done(((bf16[2916,288]{0,1:T(8,128)(2,1)}), bf16[2916,288]{0,1:T(8,128)(2,1)}) %all-reduce.28.cloned.1.call-update) | async-done | bytes 1679632
  1285.4 28.9 %all-gather.21.cloned.1.call-done = bf16[2,1458,288]{1,2,0:T(8,128)(2,1)} async-done(((bf16[1,1458,288]{1,2,0:T(8,128)(2,1)}), bf16[2,1458,288]{1,2,0:T(8,128)(2,1)}) %all-gather.21.cloned.1.call-update) | async-done | bytes 1679632 | tf_op jit(solution)/shard_map/all_gather | solution.py:43
  1330.4 120.4 %all-reduce.35 = bf16[2916,576]{0,1:T(8,128)(2,1)} all-reduce(f32[2916,576]{0,1:T(8,128)} %fusion.54), channel_id=8, replica_groups=mesh['dp'=4,'row'=4,'col'=2] {'row'}, use_global_device_ids=true, to_apply=%region_20.21.clone | all-reduce | flops 1679616 | bytes 10077696
  1452.5 12.2 multiply_reduce_fusion
  1464.7 12.8 multiply_convert_fusion
  1497.6 16.5 convolution_convert_fusion
  1531.8 35.6 %all-gather.23.cloned.1.call-done = bf16[4,729,1728]{2,1,0:T(8,128)(2,1)} async-done(((bf16[1,729,1728]{2,1,0:T(8,128)(2,1)}), bf16[4,729,1728]{2,1,0:T(8,128)(2,1)}) %all-gather.23.cloned.1.call-update) | async-done | bytes 10077712 | tf_op jit(solution)/shard_map/all_gather | solution.py:71
  1567.4 14.8 reshape.103
  1611.9 19.5 %reduce-scatter.21.cloned.1.call-done = bf16[72,2152]{1,0:T(8,128)(2,1)} async-done(((bf16[288,2152]{1,0:T(8,128)(2,1)}), bf16[72,2152]{1,0:T(8,128)(2,1)}) %reduce-scatter.21.cloned.1.call-update) | async-done | bytes 309904
  1635.2 19.0 %reduce-scatter.19.cloned.1.call-done = bf16[144,288]{1,0:T(8,128)(2,1)} async-done(((bf16[576,288]{1,0:T(8,128)(2,1)}), bf16[144,288]{1,0:T(8,128)(2,1)}) %reduce-scatter.19.cloned.1.call-update) | async-done | bytes 82960 | tf_op jit(solution)/shard_map/reduce_scatter | solution.py:242
  1655.8 64.9 %all-reduce.34.cloned.1.call-done = bf16[288,3,576]{2,1,0:T(4,128)(2,1)} async-done(((bf16[288,3,576]{2,1,0:T(4,128)(2,1)}), bf16[288,3,576]{2,1,0:T(4,128)(2,1)}) %all-reduce.34.cloned.1.call-update) | async-done | bytes 995344
  1722.6 90.7 %all-reduce.32.cloned.1.call-done = f32[2916,288]{0,1:T(8,128)} async-done(((f32[2916,288]{0,1:T(8,128)}), f32[2916,288]{0,1:T(8,128)}) %all-reduce.32.cloned.1.call-update) | async-done | bytes 3359248
  1816.4 40.5 %all-reduce.14 = (f32[6,1152]{1,0:T(8,128)S(1)}, f32[2,1152]{1,0:T(2,128)S(1)}, f32[4304]{0:T(1024)S(1)}) all-reduce(f32[6,1152]{1,0:T(8,128)S(1)} %dynamic_update_slice.18, f32[2,1152]{1,0:T(2,128)S(1)} %dynamic_update_slice.19, f32[4304]{0:T(1024)S(1)} %dynamic_update_slice.20), channel_id=1, replica_groups=mesh['dp'=4,'row'=4,'col'=2] {'dp','row','col'}, use_global_device_ids=true, to_apply=%region_33.34 | all-reduce | flops 13520 | bytes 108160 | tf_op jit(solution)/shard_map/psum | solution.py:233
  (190 shorter events, 274.6 us)
Async XLA Ops:
  7.2 665.0 %copy-start = (bf16[288,2152]{1,0:T(8,128)(2,1)S(1)}, bf16[288,2152]{1,0:T(8,128)(2,1)}, u32[]{:S(2)}) copy-start(bf16[288,2152]{1,0:T(8,128)(2,1)} %param.19) | copy-start | bytes 3718660
  7.2 48.7 %all-gather.13.cloned.1.call-start = ((), (), s32[]{:S(2)}) async-start(), calls=%async_computation.4 | async-start | bytes 2654208 | tf_op jit(solution)/shard_map/all_gather | solution.py:43
  26.0 346.4 %all-gather.17.cloned.1.call-start = ((), (), s32[]{:S(2)}) async-start(), calls=%async_computation.6 | async-start | bytes 2654208 | tf_op jit(solution)/shard_map/all_gather | solution.py:43
  76.9 184.3 %copy-start.23 = (u32[32]{0:T(128)S(1)}, u32[32]{0:T(128)}, u32[]{:S(2)}) copy-start(u32[32]{0:T(128)} %constant.92) | copy-start | bytes 388
  259.3 3.2 collective-permute-start.4
  316.2 49.1 %copy-start.13 = (bf16[576,288]{0,1:T(8,128)(2,1)S(1)}, bf16[576,288]{0,1:T(8,128)(2,1)}, u32[]{:S(2)}) copy-start(bf16[576,288]{0,1:T(8,128)(2,1)} %param.17) | copy-start | bytes 995332
  316.2 4.1 collective-permute-start
  323.5 41.8 %collective-permute-start.1 = (bf16[1458,576]{0,1:T(8,128)(2,1)S(1)}, bf16[1458,576]{0,1:T(8,128)(2,1)}, u32[]{:S(2)}, u32[]{:S(2)}) collective-permute-start(bf16[1458,576]{0,1:T(8,128)(2,1)S(1)} %maximum_select_fusion.5), channel_id=1, source_target_pairs={{0,4},{2,6},{4,0},{6,2},{1,5},{3,7},{5,1},{7,3},{8,12},{10,14},{12... | collective-permute-start | bytes 5038856 | tf_op jit(solution)/shard_map/ppermute | solution.py:89
  326.3 99.2 %all-reduce.26.cloned.1.call-start = ((), (), s32[]{:S(2)}) async-start(), calls=%async_computation.10 | async-start | bytes 3391488
  370.9 291.4 %all-gather.15.cloned.1.call-start = ((), (), s32[]{:S(2)}) async-start(), calls=%async_computation.5 | async-start | bytes 2654208 | tf_op jit(solution)/shard_map/all_gather | solution.py:43
  378.2 47.4 %copy-start.2 = (bf16[1458,288]{0,1:T(8,128)(2,1)S(1)}, bf16[1458,288]{0,1:T(8,128)(2,1)}, u32[]{:S(2)}) copy-start(bf16[1458,288]{0,1:T(8,128)(2,1)} %param.12) | copy-start | bytes 2519428
  441.6 658.6 %all-gather.19.cloned.1.call-start = ((), (), s32[]{:S(2)}) async-start(), calls=%async_computation.7 | async-start | bytes 16015360 | tf_op jit(solution)/shard_map/all_gather | solution.py:71
  660.7 246.7 %collective-permute-start.6 = (f32[21,2152]{1,0:T(8,128)S(1)}, f32[21,2152]{1,0:T(8,128)S(1)}, u32[]{:S(2)}, u32[]{:S(2)}) collective-permute-start(f32[21,2152]{1,0:T(8,128)S(1)} %slice.78), channel_id=1, source_target_pairs={{0,2},{2,4},{4,6},{1,3},{3,5},{5,7},{8,10},{10,12},{12,14},{9,11},... | collective-permute-start | bytes 542312
  685.3 222.2 %copy-start.22 = (bf16[2152]{0:T(1024)(128)(2,1)S(1)}, bf16[2152]{0:T(1024)(128)(2,1)}, u32[]{:S(2)}) copy-start(bf16[2152]{0:T(1024)(128)(2,1)} %param.20) | copy-start | bytes 12916
  906.1 18.9 %collective-permute-start.5 = (f32[21,2152]{1,0:T(8,128)S(1)}, f32[21,2152]{1,0:T(8,128)S(1)}, u32[]{:S(2)}, u32[]{:S(2)}) collective-permute-start(f32[21,2152]{1,0:T(8,128)S(1)} %slice.77), channel_id=1, source_target_pairs={{0,2},{2,4},{4,6},{1,3},{3,5},{5,7},{8,10},{10,12},{12,14},{9,11},... | collective-permute-start | bytes 542312
  954.9 265.5 %all-reduce.30.cloned.1.call-start = ((), (), s32[]{:S(2)}) async-start(), calls=%async_computation.12 | async-start | bytes 6782976
  955.4 6.7 collective-permute-start.2
  971.1 201.7 %collective-permute-start.3 = (bf16[1458,2152]{1,0:T(8,128)(2,1)}, bf16[1458,2152]{1,0:T(8,128)(2,1)}, u32[]{:S(2)}, u32[]{:S(2)}) collective-permute-start(bf16[1458,2152]{1,0:T(8,128)(2,1)} %maximum_select_fusion.1), channel_id=1, source_target_pairs={{0,4},{2,6},{4,0},{6,2},{1,5},{3,7},{5,1},{7,3},{8,12},{10,14},{12... | collective-permute-start | bytes 18825704 | tf_op jit(solution)/shard_map/ppermute | solution.py:89
  1127.7 62.3 %copy-start.25 = (bf16[288]{0:T(512)(128)(2,1)S(1)}, bf16[288]{0:T(512)(128)(2,1)}, u32[]{:S(2)}) copy-start(bf16[288]{0:T(512)(128)(2,1)} %param.22) | copy-start | bytes 1732
  1127.7 149.2 %all-reduce.28.cloned.1.call-start = ((), (), s32[]{:S(2)}) async-start(), calls=%async_computation.11 | async-start | bytes 3391488
  1189.9 87.0 %copy-start.8 = (bf16[1458,288]{0,1:T(8,128)(2,1)S(1)}, bf16[1458,288]{0,1:T(8,128)(2,1)}, u32[]{:S(2)}) copy-start(bf16[1458,288]{0,1:T(8,128)(2,1)} %param.23) | copy-start | bytes 2519428
  1190.0 124.3 %all-gather.21.cloned.1.call-start = ((), (), s32[]{:S(2)}) async-start(), calls=%async_computation.8 | async-start | bytes 2654208 | tf_op jit(solution)/shard_map/all_gather | solution.py:43
  1284.7 282.7 %all-gather.23.cloned.1.call-start = ((), (), s32[]{:S(2)}) async-start(), calls=%async_computation.9 | async-start | bytes 13189120 | tf_op jit(solution)/shard_map/all_gather | solution.py:71
  1497.2 112.9 %reduce-scatter.23.cloned.1.call-start = ((), (), s32[]{:S(2)}) async-start(), calls=%async_computation.16 | async-start | bytes 1566720
  1514.2 117.2 %reduce-scatter.21.cloned.1.call-start = ((), (), s32[]{:S(2)}) async-start(), calls=%async_computation.15 | async-start | bytes 1566720
  1524.8 129.4 %reduce-scatter.19.cloned.1.call-start = ((), (), s32[]{:S(2)}) async-start(), calls=%async_computation.3 | async-start | bytes 552960 | tf_op jit(solution)/shard_map/reduce_scatter | solution.py:242
  1531.5 189.1 %all-reduce.34.cloned.1.call-start = ((), (), s32[]{:S(2)}) async-start(), calls=%async_computation.14 | async-start | bytes 2949120
  1597.9 215.4 %all-reduce.32.cloned.1.call-start = ((), (), s32[]{:S(2)}) async-start(), calls=%async_computation.13 | async-start | bytes 6782976
  1611.9 201.4 %copy-start.15 = (f32[1458]{0:T(1024)S(1)}, f32[1458]{0:T(1024)}, u32[]{:S(2)}) copy-start(f32[1458]{0:T(1024)} %copy-done.14) | copy-start | bytes 17500
  1611.9 201.5 %copy-start.17 = (f32[1458]{0:T(1024)S(1)}, f32[1458]{0:T(1024)}, u32[]{:S(2)}) copy-start(f32[1458]{0:T(1024)} %copy-done.16) | copy-start | bytes 17500
  1611.9 201.5 %copy-start.20 = (f32[288]{0:T(512)S(1)}, f32[288]{0:T(512)}, u32[]{:S(2)}) copy-start(f32[288]{0:T(512)} %copy-done.19) | copy-start | bytes 3460
  1813.3 61.0 %copy-start.1 = (bf16[288,2152]{1,0:T(8,128)(2,1)S(1)}, bf16[288,2152]{1,0:T(8,128)(2,1)}, u32[]{:S(2)}) copy-start(bf16[288,2152]{1,0:T(8,128)(2,1)} %param.19) | copy-start | bytes 3718660
  (17 other events, 262.8 us)
Sparse Core Ops, SparseCore 0:
  26.1 29.7 all-gather.12
  326.5 28.4 all-gather.16
  371.0 54.5 all-reduce.25
  441.7 29.0 all-gather.14
  955.0 145.0 all-gather.18
  1127.8 92.5 all-reduce.29
  1222.7 54.1 all-reduce.27
  1284.8 29.4 all-gather.20
  1497.3 70.0 all-gather.22
  1569.5 30.2 reduce-scatter.22
  1602.1 29.1 reduce-scatter.20
  1634.1 20.1 reduce-scatter.18
  1656.6 64.0 all-reduce.33
  1722.9 90.4 all-reduce.31
